TPU v7x, 512 devices: a whole 4x8x8 slice. The times are simulated.
512 devices in a mesh: doc: 32 (over z, x), cent: 16 (over y, core).
Axes of the slice: x: 4, y: 8, z: 8, core: 2. Of those that a mesh axis runs over, the one named last changes fastest.
Arguments:
- rows: bfloat16 [65536, 1024], P('doc'), may hold values from -30 to 30
- centroids: bfloat16 [8192, 1024], P('cent'), may hold values from -16 to 16
Outputs:
- new_centroids: float32 [8192, 1024], P(('cent', 'doc'))
All inputs are finite; a program needn't handle non-finite values.
Results may differ from a plain program's by a relative error of at most 0.0009.
Values sent between devices are 32-bit elements; how exact they have to be, the bound alone decides.
A program may use at most 64 MiB of HBM per device.

v0:
```python
import math
import jax
import jax.numpy as jnp
from jax import lax
from jax.sharding import PartitionSpec as P


def on_device(rows, centroids):
    scale = 1.0 / (0.6 * math.sqrt(rows.shape[1]))
    logits = jnp.einsum("rd,kd->rk", rows, centroids, preferred_element_type=jnp.float32) * scale
    local_max = jnp.max(logits, axis=1)
    highest = lax.pmax(local_max, "cent")
    total = lax.psum(jnp.sum(jnp.exp(logits - highest[:, None]), axis=1), "cent")
    lse = highest + jnp.log(total)
    resp = jnp.exp(logits - lse[:, None]).astype(jnp.bfloat16)
    sums = jnp.einsum("rk,rd->kd", resp, rows, preferred_element_type=jnp.float32)
    totals = jnp.sum(resp, axis=0, dtype=jnp.float32)
    share = centroids.shape[0] // lax.axis_size("doc")
    start = lax.axis_index("doc") * share
    own_rows = lax.dynamic_slice_in_dim(centroids, start, share, 0).astype(jnp.float32)
    whole_sums, whole_totals = lax.psum((sums, totals), "doc")
    part_sums = lax.dynamic_slice_in_dim(whole_sums, start, share, 0)
    part_totals = lax.dynamic_slice_in_dim(whole_totals, start, share, 0)
    return (part_sums + own_rows) / (part_totals[:, None] + 1.0)


def solution(mesh):
    return jax.shard_map(
        on_device,
        mesh=mesh,
        in_specs=(P("doc", None), P("cent", None)),
        out_specs=P(("cent", "doc"), None),
        check_vma=False,
    )
```

profile of v0, /device:TPU:8, one launch (start us, length us, event | category | flops | bytes accessed | tf_op | source)
XLA Modules:
  0.0 250.1 jit_solution(16175770408922332020)
XLA Ops:
  6.5 0.0 all-reduce.2.cloned.1.call-start
  6.5 6.8 %multiply_reduce_fusion = (f32[2048]{0:T(1024)S(1)}, f32[2048,512]{0,1:T(8,128)}) fusion(bf16[2048,1024]{1,0:T(8,128)(2,1)} %param.2, bf16[512,1024]{1,0:T(8,128)(2,1)} %param.3), kind=kOutput, calls=%fused_computation.3 | convolution fusion | flops 2149578752 | bytes 9445376 | tf_op jit(solution)/shard_map/rd,kd->rk/dot_general | solution.py:10
  13.3 26.3 %pmax.7 = f32[2048]{0:T(1024)S(1)} all-reduce(f32[2048]{0:T(1024)S(1)} %get-tuple-element.5), channel_id=1, replica_groups=mesh['doc'=32,'cent'=16] {'cent'}, use_global_device_ids=true, to_apply=%region_1.0 | all-reduce | flops 2048 | bytes 16384 | tf_op jit(solution)/shard_map/pmax | solution.py:12
  39.7 2.9 %exponential_reduce_fusion = f32[2048]{0:T(1024)S(1)} fusion(f32[2048,512]{0,1:T(8,128)} %get-tuple-element.6, f32[2048]{0:T(1024)S(1)} %pmax.7), kind=kLoop, calls=%fused_computation.2 | loop fusion | flops 3143680 | bytes 4210688 | tf_op jit(solution)/shard_map/reduce_sum | solution.py:13
  42.6 24.0 %psum.21 = f32[2048]{0:T(1024)S(1)} all-reduce(f32[2048]{0:T(1024)S(1)} %exponential_reduce_fusion), channel_id=1, replica_groups=mesh['doc'=32,'cent'=16] {'cent'}, use_global_device_ids=true, to_apply=%region_3.0 | all-reduce | flops 2048 | bytes 16384 | tf_op jit(solution)/shard_map/psum | solution.py:13
  66.6 7.1 %fusion = f32[512,1024]{1,0:T(8,128)} fusion(bf16[2048,1024]{1,0:T(8,128)(2,1)} %param.2, f32[2048,512]{0,1:T(8,128)} %get-tuple-element.6, f32[2048]{0:T(1024)S(1)} %log_add_fusion), kind=kOutput, calls=%fused_computation.4 | convolution fusion | flops 2150629376 | bytes 10493952 | tf_op jit(solution)/shard_map/rk,rd->kd/dot_general | solution.py:16
  73.8 0.0 all-reduce.2.cloned.1.call-update
  73.8 2.9 %convert_reduce_fusion = f32[512]{0:T(512)S(1)} fusion(f32[2048]{0:T(1024)S(1)} %log_add_fusion, f32[2048,512]{0,1:T(8,128)} %get-tuple-element.6), kind=kLoop, calls=%fused_computation | loop fusion | flops 5242368 | bytes 4204544 | tf_op jit(solution)/shard_map/reduce_sum | solution.py:17
  76.8 78.6 %psum.23 = f32[512]{0:T(512)S(1)} all-reduce(f32[512]{0:T(512)S(1)} %convert_reduce_fusion), channel_id=1, replica_groups=mesh['doc'=32,'cent'=16] {'doc'}, use_global_device_ids=true, to_apply=%region_6.0 | all-reduce | flops 512 | bytes 4096 | tf_op jit(solution)/shard_map/psum | solution.py:21
  155.4 0.1 dynamic-slice_add_fusion
  155.5 86.3 %all-reduce.2.cloned.1.call-done = f32[512,1024]{1,0:T(8,128)} async-done(((f32[512,1024]{1,0:T(8,128)}), f32[512,1024]{1,0:T(8,128)}) %all-reduce.2.cloned.1.call-update) | async-done | bytes 2097168 | tf_op jit(solution)/shard_map/psum | solution.py:21
  241.7 1.5 add_divide_fusion
  (1 shorter events, 0.0 us)
Async XLA Ops:
  6.5 235.2 %all-reduce.2.cloned.1.call-start = ((), (), s32[]{:S(2)}) async-start(), calls=%async_computation | async-start | bytes 4194304 | tf_op jit(solution)/shard_map/psum | solution.py:21
Sparse Core Ops, SparseCore 0:
  73.9 167.7 all-reduce.1
where the time goes:
time: 250 us
  blocking collectives  129 us (52%)
  waiting for transfers between devices  86.3 us (35%)
  matrix products  13.9 us (6%)
  between operations  13.4 us (5%)
  other arithmetic  7.48 us (3%)
    psum x1, waiting for transfers between devices, on_device(): whole_sums, whole_totals = lax.psum((sums, totals), 'doc')  86.3 us
    psum x1, blocking collectives, on_device(): whole_sums, whole_totals = lax.psum((sums, totals), 'doc')  78.6 us
    pmax x1, blocking collectives, on_device(): highest = lax.pmax(local_max, 'cent')  26.3 us
    psum x1, blocking collectives, on_device(): lax.psum(jnp.sum(jnp.exp(logits - highest[:, None]), axis=1), 'cent')  24 us
    dot_general x1, matrix products, on_device(): jnp.einsum('rk,rd->kd', resp, rows, preferred_element_type=jnp.float32)  7.14 us
    dot_general x1, matrix products, on_device(): jnp.einsum('rd,kd->rk', rows, centroids, preferred_element_type=jnp.float32)  6.78 us
  transfers between devices with their start and end apart: 1, of which 1 were waited for; matrix products, arithmetic and copies ran while one was open for 1% of the time, Pallas kernels for 0%

commit v1 on v0

--- a/solution.py
+++ b/solution.py
@@ -10,7 +10,9 @@
     logits = jnp.einsum("rd,kd->rk", rows, centroids, preferred_element_type=jnp.float32) * scale
     local_max = jnp.max(logits, axis=1)
     highest = lax.pmax(local_max, "cent")
-    total = lax.psum(jnp.sum(jnp.exp(logits - highest[:, None]), axis=1), "cent")
+    total = jnp.sum(
+        lax.all_gather(jnp.sum(jnp.exp(logits - highest[:, None]), axis=1), "cent"), axis=0
+    )
     lse = highest + jnp.log(total)
     resp = jnp.exp(logits - lse[:, None]).astype(jnp.bfloat16)
     sums = jnp.einsum("rk,rd->kd", resp, rows, preferred_element_type=jnp.float32)

time: 250 us -> 241 us (0.964)
  blocking collectives: 129 us -> 123 us
  waiting for transfers between devices: 86.3 us -> 83.5 us
    psum x1 -> x0, blocking collectives: 24 us -> none  [on_device(): lax.psum(jnp.sum(jnp.exp(logits - highest[:, None]), axis=1), 'cent')]
    all_gather x0 -> x1, blocking collectives: none -> 18 us  [on_device(): lax.all_gather(jnp.sum(jnp.exp(logits - highest[:, None]), axis=1), 'cent')]
    psum x1, waiting for transfers between devices: 86.3 us -> 83.5 us  [on_device(): whole_sums, whole_totals = lax.psum((sums, totals), 'doc')]
where the time goes in v1:
time: 241 us
  blocking collectives  123 us (51%)
  waiting for transfers between devices  83.5 us (35%)
  matrix products  13.9 us (6%)
  between operations  13.4 us (6%)
  other arithmetic  7.51 us (3%)
    psum x1, waiting for transfers between devices, on_device(): whole_sums, whole_totals = lax.psum((sums, totals), 'doc')  83.5 us
    psum x1, blocking collectives, on_device(): whole_sums, whole_totals = lax.psum((sums, totals), 'doc')  78.5 us
    pmax x1, blocking collectives, on_device(): highest = lax.pmax(local_max, 'cent')  26.3 us
    all_gather x1, blocking collectives, on_device(): lax.all_gather(jnp.sum(jnp.exp(logits - highest[:, None]), axis=1), 'cent')  18 us
    dot_general x1, matrix products, on_device(): jnp.einsum('rk,rd->kd', resp, rows, preferred_element_type=jnp.float32)  7.14 us
    dot_general x1, matrix products, on_device(): jnp.einsum('rd,kd->rk', rows, centroids, preferred_element_type=jnp.float32)  6.78 us
  transfers between devices with their start and end apart: 1, of which 1 were waited for; matrix products, arithmetic and copies ran while one was open for 1% of the time, Pallas kernels for 0%

profile of v1, /device:TPU:8, one launch (start us, length us, event | category | flops | bytes accessed | tf_op | source)
XLA Modules:
  0.0 241.2 jit_solution(14324580828702818644)
XLA Ops:
  6.5 0.0 all-reduce.2.cloned.1.call-start
  6.5 6.8 %multiply_reduce_fusion = (f32[2048]{0:T(1024)S(1)}, f32[2048,512]{0,1:T(8,128)}) fusion(bf16[2048,1024]{1,0:T(8,128)(2,1)} %param.2, bf16[512,1024]{1,0:T(8,128)(2,1)} %param.3), kind=kOutput, calls=%fused_computation.3 | convolution fusion | flops 2149578752 | bytes 9445376 | tf_op jit(solution)/shard_map/rd,kd->rk/dot_general | solution.py:10
  13.3 26.3 %pmax.7 = f32[2048]{0:T(1024)S(1)} all-reduce(f32[2048]{0:T(1024)S(1)} %get-tuple-element.5), channel_id=1, replica_groups=mesh['doc'=32,'cent'=16] {'cent'}, use_global_device_ids=true, to_apply=%region_1.0 | all-reduce | flops 2048 | bytes 16384 | tf_op jit(solution)/shard_map/pmax | solution.py:12
  39.7 2.9 %exponential_reduce_fusion = f32[2048]{0:T(1024)S(1)} fusion(f32[2048,512]{0,1:T(8,128)} %get-tuple-element.6, f32[2048]{0:T(1024)S(1)} %pmax.7), kind=kLoop, calls=%fused_computation.2 | loop fusion | flops 3143680 | bytes 4210688 | tf_op jit(solution)/shard_map/reduce_sum | solution.py:14
  42.6 18.0 %all-gather = f32[32768]{0:T(1024)S(1)} all-gather(f32[2048]{0:T(1024)S(1)} %exponential_reduce_fusion), channel_id=2, replica_groups=mesh['doc'=32,'cent'=16] {'cent'}, dimensions={0}, use_global_device_ids=true | all-gather | bytes 139264 | tf_op jit(solution)/shard_map/all_gather | solution.py:14
  60.6 7.1 %fusion = f32[512,1024]{1,0:T(8,128)} fusion(bf16[2048,1024]{1,0:T(8,128)(2,1)} %param.2, f32[2048,512]{0,1:T(8,128)} %get-tuple-element.6, f32[2048]{0:T(1024)S(1)} %log_add_fusion), kind=kOutput, calls=%fused_computation.4 | convolution fusion | flops 2150629376 | bytes 10493952 | tf_op jit(solution)/shard_map/rk,rd->kd/dot_general | solution.py:18
  67.8 0.0 all-reduce.2.cloned.1.call-update
  67.8 2.9 %convert_reduce_fusion = f32[512]{0:T(512)S(1)} fusion(f32[2048]{0:T(1024)S(1)} %log_add_fusion, f32[2048,512]{0,1:T(8,128)} %get-tuple-element.6), kind=kLoop, calls=%fused_computation | loop fusion | flops 5242368 | bytes 4204544 | tf_op jit(solution)/shard_map/reduce_sum | solution.py:19
  70.7 78.5 %psum.15 = f32[512]{0:T(512)S(1)} all-reduce(f32[512]{0:T(512)S(1)} %convert_reduce_fusion), channel_id=1, replica_groups=mesh['doc'=32,'cent'=16] {'doc'}, use_global_device_ids=true, to_apply=%region_6.0 | all-reduce | flops 512 | bytes 4096 | tf_op jit(solution)/shard_map/psum | solution.py:23
  149.2 0.1 dynamic-slice_add_fusion
  149.3 83.5 %all-reduce.2.cloned.1.call-done = f32[512,1024]{1,0:T(8,128)} async-done(((f32[512,1024]{1,0:T(8,128)}), f32[512,1024]{1,0:T(8,128)}) %all-reduce.2.cloned.1.call-update) | async-done | bytes 2097168 | tf_op jit(solution)/shard_map/psum | solution.py:23
  232.8 1.5 add_divide_fusion
  (3 shorter events, 0.1 us)
Async XLA Ops:
  6.5 226.3 %all-reduce.2.cloned.1.call-start = ((), (), s32[]{:S(2)}) async-start(), calls=%async_computation | async-start | bytes 4194304 | tf_op jit(solution)/shard_map/psum | solution.py:23
Sparse Core Ops, SparseCore 0:
  67.9 164.8 all-reduce.1
